TPU v7x, 32 devices: a whole 2x2x4 slice. The times are simulated.
32 devices in a mesh: ctx: 4 (over y, core), tp: 4 (over z), dp: 2 (over x).
Axes of the slice: x: 2, y: 2, z: 4, core: 2. Of those that a mesh axis runs over, the one named last changes fastest.
Arguments:
- tokens: bfloat16 [3072, 3584], P(('dp', 'ctx'), 'tp'), may hold values from -6 to 6
- expert_ids: int32 [3072, 8], P(('dp', 'ctx')), may hold values from 0 to 255, all different within a row; in each aligned block of 384 rows (0 to 383, 384 to 767, ...) at most 24 rows name the same one
- gate_codes: int32 [3072, 8], P(('dp', 'ctx')), may hold values from 1 to 32767
- up_weight: bfloat16 [4, 3584, 1024], P('ctx', 'tp', 'dp'), may hold values from -0.09375 to 0.09375
- down_weight: bfloat16 [4, 1024, 3584], P('ctx', 'dp', 'tp'), may hold values from -0.1875 to 0.1875
- cotangent: bfloat16 [3072, 3584], P(('dp', 'ctx'), 'tp'), may hold values from -6 to 6
Outputs:
- mixed: bfloat16 [3072, 3584], P(('dp', 'ctx'), 'tp')
- grad_tokens: bfloat16 [3072, 3584], P(('dp', 'ctx'), 'tp')
- grad_up: bfloat16 [4, 3584, 1024], P('ctx', 'tp', 'dp')
- grad_down: bfloat16 [4, 1024, 3584], P('ctx', 'dp', 'tp')
Inputs may be any that keep to these rules, and one draw needn't show every extreme that they name: `expert_ids`: each row names 8 different experts; among the 384 rows of one device no expert is named more than 24 times.
All inputs are finite; a program needn't handle non-finite values.
Results may differ from a plain program's by a relative error of at most 0.0066.
Values may be sent and summed in bfloat16 or wider, within the bound.
A program may use at most 64 MiB of HBM per device.

v0:
```python
import jax
import jax.numpy as jnp
from jax import lax
from jax.sharding import PartitionSpec as P


def place_slots(expert_ids, gate_codes, experts, capacity):
    rows_count, picks = expert_ids.shape
    flat_ids = expert_ids.reshape(-1)
    one_hot = (flat_ids[:, None] == jnp.arange(experts, dtype=jnp.int32)[None, :]).astype(jnp.int32)
    before = jnp.cumsum(one_hot, axis=0) - one_hot
    slot_rank = jnp.sum(before * one_hot, axis=1)
    inside = flat_ids < experts
    target = jnp.where(inside, flat_ids * capacity + slot_rank, experts * capacity)
    source = jnp.arange(rows_count * picks, dtype=jnp.int32) // picks
    slot_token = (
        jnp.full((experts * capacity,), rows_count, jnp.int32).at[target].set(source, mode="drop")
    )
    weights = gate_codes.reshape(-1).astype(jnp.float32) / 32768.0
    gate_slot = jnp.zeros((experts * capacity,), jnp.float32).at[target].set(weights, mode="drop")
    return (slot_token, gate_slot)


def silu_grad(values):
    sigma = jax.nn.sigmoid(values)
    return sigma * (1.0 + values * (1.0 - sigma))


def body(tokens, expert_ids, gate_codes, up_weight, down_weight, cotangent):
    sources = lax.axis_size("ctx")
    rows_count, features = tokens.shape
    capacity = rows_count // 16
    slot_token, gate_slot = place_slots(expert_ids, gate_codes, sources, capacity)
    padded_x = jnp.concatenate([tokens, jnp.zeros((1, features), tokens.dtype)], axis=0)
    outgoing = padded_x[slot_token].reshape(sources, capacity, features)
    arrived = lax.all_to_all(outgoing, "ctx", split_axis=0, concat_axis=0, tiled=True).reshape(
        sources * capacity, features
    )
    w_up, w_down = (
        lax.all_gather(up_weight[0], "dp", axis=1, tiled=True),
        lax.all_gather(down_weight[0], "dp", axis=0, tiled=True),
    )
    hidden = lax.psum(jnp.dot(arrived, w_up, preferred_element_type=jnp.float32), "tp")
    active = jax.nn.silu(hidden).astype(jnp.bfloat16)
    produced = jnp.dot(active, w_down, preferred_element_type=jnp.float32).astype(jnp.bfloat16)
    returned = lax.all_to_all(
        produced.reshape(sources, capacity, features),
        "ctx",
        split_axis=0,
        concat_axis=0,
        tiled=True,
    ).reshape(sources * capacity, features)
    mixed = (
        jnp.zeros((rows_count + 1, features), jnp.float32)
        .at[slot_token]
        .add(gate_slot[:, None] * returned.astype(jnp.float32))
    )
    mixed = mixed[:rows_count].astype(jnp.bfloat16)
    padded_c = jnp.concatenate([cotangent, jnp.zeros((1, features), cotangent.dtype)], axis=0)
    grad_send = (gate_slot[:, None] * padded_c[slot_token].astype(jnp.float32)).astype(jnp.bfloat16)
    grad_rows = lax.all_to_all(
        grad_send.reshape(sources, capacity, features),
        "ctx",
        split_axis=0,
        concat_axis=0,
        tiled=True,
    ).reshape(sources * capacity, features)
    contract_last = (((1,), (1,)), ((), ()))
    contract_first = (((0,), (0,)), ((), ()))
    grad_act = lax.psum(
        lax.dot_general(grad_rows, w_down, contract_last, preferred_element_type=jnp.float32), "tp"
    )
    grad_hid = (grad_act * silu_grad(hidden)).astype(jnp.bfloat16)
    grad_in = lax.dot_general(
        grad_hid, w_up, contract_last, preferred_element_type=jnp.float32
    ).astype(jnp.bfloat16)
    back_rows = lax.all_to_all(
        grad_in.reshape(sources, capacity, features), "ctx", split_axis=0, concat_axis=0, tiled=True
    ).reshape(sources * capacity, features)
    grad_tokens = (
        jnp.zeros((rows_count + 1, features), jnp.float32)
        .at[slot_token]
        .add(back_rows.astype(jnp.float32))
    )
    grad_tokens = grad_tokens[:rows_count].astype(jnp.bfloat16)
    part_up = lax.dot_general(arrived, grad_hid, contract_first, preferred_element_type=jnp.float32)
    part_down = lax.dot_general(
        active, grad_rows, contract_first, preferred_element_type=jnp.float32
    )
    grad_up, grad_down = (
        lax.psum_scatter(
            part_up.astype(jnp.bfloat16), "dp", scatter_dimension=1, tiled=True
        ).astype(jnp.float32),
        lax.psum_scatter(
            part_down.astype(jnp.bfloat16), "dp", scatter_dimension=0, tiled=True
        ).astype(jnp.float32),
    )
    return (
        mixed,
        grad_tokens,
        grad_up.astype(jnp.bfloat16)[None],
        grad_down.astype(jnp.bfloat16)[None],
    )


def solution(mesh):
    return jax.shard_map(
        body,
        mesh=mesh,
        in_specs=(
            P(("dp", "ctx"), "tp"),
            P(("dp", "ctx"), None),
            P(("dp", "ctx"), None),
            P("ctx", "tp", "dp"),
            P("ctx", "dp", "tp"),
            P(("dp", "ctx"), "tp"),
        ),
        out_specs=(
            P(("dp", "ctx"), "tp"),
            P(("dp", "ctx"), "tp"),
            P("ctx", "tp", "dp"),
            P("ctx", "dp", "tp"),
        ),
        check_vma=False,
    )
```

profile of v0, /device:TPU:0, one launch (start us, length us, event | category | flops | bytes accessed | tf_op | source)
XLA Modules:
  0.0 190.8 jit_solution(14327130908680088390)
XLA Ops:
  7.2 0.7 all-gather.5.cloned.1.call-update
  8.0 0.7 all-gather.7.cloned.1.call-update
  9.1 0.2 copy.10
  9.7 1.2 reduce-window.6
  10.9 0.2 slice_reduce_fusion
  11.1 0.2 reduce-window.9
  11.6 11.8 %scatter_custom_fusion = s32[96]{0:T(128)S(1)} fusion(s32[3072]{0:T(1024)S(1)} %bitcast.64, s32[3072]{0:T(1024)S(1)} %add_select_fusion, s32[]{:T(128)} %constant.17.clone.1), kind=kCustom, calls=%fused_computation.56 | custom fusion | bytes 388 | tf_op jit(solution)/shard_map/scatter | solution.py:17
  23.4 1.5 gather_fusion
  24.9 4.3 %all-to-all-start = ((bf16[4,24,896]{2,1,0:T(8,128)(2,1)}), bf16[4,24,896]{2,1,0:T(8,128)(2,1)S(1)}, u32[]{:S(2)}, u32[]{:S(2)}) async-start(bf16[4,24,896]{2,1,0:T(8,128)(2,1)} %bitcast.3), calls=%async_computation | async-start | bytes 344064 | tf_op jit(solution)/shard_map/all_to_all | solution.py:36
  29.4 11.8 %scatter_custom_fusion.1 = f32[96]{0:T(128)S(1)} fusion(s32[3072]{0:T(1024)S(1)} %bitcast.65, f32[3072]{0:T(1024)S(1)} %reshape.139, f32[]{:T(128)} %constant.15.clone.1), kind=kCustom, calls=%fused_computation.54 | custom fusion | bytes 388 | tf_op jit(solution)/shard_map/scatter | solution.py:20
  41.3 0.8 gather_fusion.1
  42.1 0.8 fusion.19
  42.9 3.4 %all-to-all-start.2 = ((bf16[4,24,896]{2,1,0:T(8,128)(2,1)}), bf16[4,24,896]{2,1,0:T(8,128)(2,1)S(1)}, u32[]{:S(2)}, u32[]{:S(2)}) async-start(bf16[4,24,896]{2,1,0:T(8,128)(2,1)} %fusion.19), calls=%async_computation.2 | async-start | bytes 344064 | tf_op jit(solution)/shard_map/all_to_all | solution.py:61
  46.3 2.7 %fusion.6 = f32[96,1024]{1,0:T(8,128)} fusion(bf16[96,896]{1,0:T(8,128)(2,1)S(1)} %bitcast.56, bf16[1,896,1024]{2,1,0:T(8,128)(2,1)} %all-gather.5.cloned.1.call-done), kind=kOutput, calls=%fused_computation.12 | convolution fusion | flops 176160768 | bytes 2400256 | tf_op jit(solution)/shard_map/dot_general | solution.py:43
  49.0 2.3 %all-to-all-done.2 = bf16[4,24,896]{2,1,0:T(8,128)(2,1)S(1)} async-done(((bf16[4,24,896]{2,1,0:T(8,128)(2,1)}), bf16[4,24,896]{2,1,0:T(8,128)(2,1)S(1)}, u32[]{:S(2)}, u32[]{:S(2)}) %all-to-all-start.2) | async-done | bytes 172064 | tf_op jit(solution)/shard_map/all_to_all | solution.py:61
  51.3 22.8 %all-gather.7.cloned.1.call-done = bf16[1,1024,896]{2,1,0:T(8,128)(2,1)} async-done(((bf16[1,512,896]{2,1,0:T(8,128)(2,1)}), bf16[1,1024,896]{2,1,0:T(8,128)(2,1)}) %all-gather.7.cloned.1.call-update) | async-done | bytes 1835024 | tf_op jit(solution)/shard_map/all_gather | solution.py:41
  74.1 2.9 %fusion = f32[96,1024]{1,0:T(8,128)} fusion(bf16[96,896]{1,0:T(8,128)(2,1)S(1)} %bitcast.58, bf16[1,1024,896]{2,1,0:T(8,128)(2,1)} %all-gather.7.cloned.1.call-done), kind=kOutput, calls=%fused_computation.6 | convolution fusion | flops 176160768 | bytes 2400256 | tf_op jit(solution)/shard_map/dot_general | solution.py:71
  77.2 44.0 %all-reduce.5.cloned.1.call-done = (f32[96,1024]{1,0:T(8,128)}, f32[96,1024]{1,0:T(8,128)}) async-done(((f32[96,1024]{1,0:T(8,128)}, f32[96,1024]{1,0:T(8,128)}), (f32[96,1024]{1,0:T(8,128)}, f32[96,1024]{1,0:T(8,128)})) %all-reduce.5.cloned.1.call-update) | async-done | bytes 786448 | tf_op jit(solution)/shard_map/psum | solution.py:43
  121.2 3.0 %convolution_convert_fusion = bf16[1024,896]{1,0:T(8,128)(2,1)} fusion(bf16[96,896]{1,0:T(8,128)(2,1)S(1)} %bitcast.59, f32[96,1024]{1,0:T(8,128)} %get-tuple-element.4), kind=kOutput, calls=%fused_computation.14 | convolution fusion | flops 177569792 | bytes 2400256 | tf_op jit(solution)/shard_map/dot_general | solution.py:87
  124.4 1.9 %convolution_convert_fusion.1 = bf16[896,1024]{1,0:T(8,128)(2,1)} fusion(bf16[96,896]{1,0:T(8,128)(2,1)S(1)} %bitcast.57, bf16[96,1024]{1,0:T(8,128)(2,1)S(1)} %multiply_convert_fusion), kind=kOutput, calls=%fused_computation.15 | convolution fusion | flops 177078272 | bytes 2203648 | tf_op jit(solution)/shard_map/dot_general | solution.py:86
  126.4 2.8 %fusion.11 = bf16[96,896]{1,0:T(8,128)(2,1)} fusion(bf16[1,1024,896]{2,1,0:T(8,128)(2,1)} %all-gather.7.cloned.1.call-done, f32[96,1024]{1,0:T(8,128)S(1)} %copy-done.1), kind=kOutput, calls=%fused_computation.19 | convolution fusion | flops 176738304 | bytes 2400256 | tf_op jit(solution)/shard_map/dot_general | solution.py:45
  129.1 3.4 %all-to-all-start.1 = ((bf16[4,24,896]{2,1,0:T(8,128)(2,1)}), bf16[4,24,896]{2,1,0:T(8,128)(2,1)S(1)}, u32[]{:S(2)}, u32[]{:S(2)}) async-start(bf16[4,24,896]{2,1,0:T(8,128)(2,1)} %bitcast.7), calls=%async_computation.1 | async-start | bytes 344064 | tf_op jit(solution)/shard_map/all_to_all | solution.py:46
  132.5 1.3 fusion.8
  133.8 3.7 %all-to-all-done.1 = bf16[4,24,896]{2,1,0:T(8,128)(2,1)S(1)} async-done(((bf16[4,24,896]{2,1,0:T(8,128)(2,1)}), bf16[4,24,896]{2,1,0:T(8,128)(2,1)S(1)}, u32[]{:S(2)}, u32[]{:S(2)}) %all-to-all-start.1) | async-done | bytes 172064 | tf_op jit(solution)/shard_map/all_to_all | solution.py:46
  137.5 3.3 %all-to-all-start.3 = ((bf16[4,24,896]{2,1,0:T(8,128)(2,1)}), bf16[4,24,896]{2,1,0:T(8,128)(2,1)S(1)}, u32[]{:S(2)}, u32[]{:S(2)}) async-start(bf16[4,24,896]{2,1,0:T(8,128)(2,1)} %bitcast.11), calls=%async_computation.3 | async-start | bytes 344064 | tf_op jit(solution)/shard_map/all_to_all | solution.py:77
  140.8 1.8 scatter_custom_fusion.2
  142.6 0.9 slice.29
  143.6 2.3 %all-to-all-done.3 = bf16[4,24,896]{2,1,0:T(8,128)(2,1)S(1)} async-done(((bf16[4,24,896]{2,1,0:T(8,128)(2,1)}), bf16[4,24,896]{2,1,0:T(8,128)(2,1)S(1)}, u32[]{:S(2)}, u32[]{:S(2)}) %all-to-all-start.3) | async-done | bytes 172064 | tf_op jit(solution)/shard_map/all_to_all | solution.py:77
  145.9 1.7 scatter_custom_fusion.3
  147.6 0.9 slice.28
  148.5 4.1 %reduce-scatter.5.cloned.1.call-done = bf16[512,896]{1,0:T(8,128)(2,1)} async-done(((bf16[1024,896]{1,0:T(8,128)(2,1)}), bf16[512,896]{1,0:T(8,128)(2,1)}) %reduce-scatter.5.cloned.1.call-update) | async-done | bytes 917520 | tf_op jit(solution)/shard_map/reduce_scatter | solution.py:94
  152.5 31.7 %reduce-scatter.3.cloned.1.call-done = bf16[896,512]{1,0:T(8,128)(2,1)} async-done(((bf16[896,1024]{1,0:T(8,128)(2,1)}), bf16[896,512]{1,0:T(8,128)(2,1)}) %reduce-scatter.3.cloned.1.call-update) | async-done | bytes 917520 | tf_op jit(solution)/shard_map/reduce_scatter | solution.py:91
  (46 shorter events, 1.9 us)
Async XLA Ops:
  7.2 1.5 copy-start.5
  7.2 4.3 %copy-start.2 = (bf16[384,896]{1,0:T(8,128)(2,1)S(1)}, bf16[384,896]{1,0:T(8,128)(2,1)}, u32[]{:S(2)}) copy-start(bf16[384,896]{1,0:T(8,128)(2,1)} %param.6) | copy-start | bytes 2064388
  7.2 39.1 %all-gather.5.cloned.1.call-start = ((), (), s32[]{:S(2)}) async-start(), calls=%async_computation.8 | async-start | bytes 2752512 | tf_op jit(solution)/shard_map/all_gather | solution.py:40
  7.9 66.2 %all-gather.7.cloned.1.call-start = ((), (), s32[]{:S(2)}) async-start(), calls=%async_computation.9 | async-start | bytes 2752512 | tf_op jit(solution)/shard_map/all_gather | solution.py:41
  9.7 19.4 %copy-start.6 = (s32[384,8]{0,1:T(8,128)S(1)}, s32[384,8]{0,1:T(8,128)}, u32[]{:S(2)}) copy-start(s32[384,8]{0,1:T(8,128)} %param.8) | copy-start | bytes 36868
  11.5 29.8 %copy-start.3 = (bf16[384,896]{1,0:T(8,128)(2,1)S(1)}, bf16[384,896]{1,0:T(8,128)(2,1)}, u32[]{:S(2)}) copy-start(bf16[384,896]{1,0:T(8,128)(2,1)} %param.11) | copy-start | bytes 2064388
  24.9 18.0 %all-to-all-start = ((bf16[4,24,896]{2,1,0:T(8,128)(2,1)}), bf16[4,24,896]{2,1,0:T(8,128)(2,1)S(1)}, u32[]{:S(2)}, u32[]{:S(2)}) async-start(bf16[4,24,896]{2,1,0:T(8,128)(2,1)} %bitcast.3), calls=%async_computation | async-start | bytes 344064 | tf_op jit(solution)/shard_map/all_to_all | solution.py:36
  42.9 8.4 %all-to-all-start.2 = ((bf16[4,24,896]{2,1,0:T(8,128)(2,1)}), bf16[4,24,896]{2,1,0:T(8,128)(2,1)S(1)}, u32[]{:S(2)}, u32[]{:S(2)}) async-start(bf16[4,24,896]{2,1,0:T(8,128)(2,1)} %fusion.19), calls=%async_computation.2 | async-start | bytes 344064 | tf_op jit(solution)/shard_map/all_to_all | solution.py:61
  46.3 74.9 %all-reduce.5.cloned.1.call-start = ((), (), s32[]{:S(2)}) async-start(), calls=%async_computation.10 | async-start | bytes 1572864 | tf_op jit(solution)/shard_map/psum | solution.py:43
  77.1 75.4 %reduce-scatter.5.cloned.1.call-start = ((), (), s32[]{:S(2)}) async-start(), calls=%async_computation.7 | async-start | bytes 2752512 | tf_op jit(solution)/shard_map/reduce_scatter | solution.py:94
  121.2 3.1 %copy-start.1 = (f32[96,1024]{1,0:T(8,128)S(1)}, f32[96,1024]{1,0:T(8,128)}, u32[]{:S(2)}) copy-start(f32[96,1024]{1,0:T(8,128)} %get-tuple-element.4) | copy-start | bytes 1179652
  121.2 3.1 %copy-start.4 = (f32[96,1024]{1,0:T(8,128)S(1)}, f32[96,1024]{1,0:T(8,128)}, u32[]{:S(2)}) copy-start(f32[96,1024]{1,0:T(8,128)} %get-tuple-element.5) | copy-start | bytes 1179652
  124.2 60.1 %reduce-scatter.3.cloned.1.call-start = ((), (), s32[]{:S(2)}) async-start(), calls=%async_computation.6 | async-start | bytes 2752512 | tf_op jit(solution)/shard_map/reduce_scatter | solution.py:91
  126.4 6.1 %copy-start = (bf16[1,896,1024]{2,1,0:T(8,128)(2,1)S(1)}, bf16[1,896,1024]{2,1,0:T(8,128)(2,1)}, u32[]{:S(2)}) copy-start(bf16[1,896,1024]{2,1,0:T(8,128)(2,1)} %all-gather.5.cloned.1.call-done) | copy-start | bytes 5505028
  129.1 8.4 %all-to-all-start.1 = ((bf16[4,24,896]{2,1,0:T(8,128)(2,1)}), bf16[4,24,896]{2,1,0:T(8,128)(2,1)S(1)}, u32[]{:S(2)}, u32[]{:S(2)}) async-start(bf16[4,24,896]{2,1,0:T(8,128)(2,1)} %bitcast.7), calls=%async_computation.1 | async-start | bytes 344064 | tf_op jit(solution)/shard_map/all_to_all | solution.py:46
  137.5 8.4 %all-to-all-start.3 = ((bf16[4,24,896]{2,1,0:T(8,128)(2,1)}), bf16[4,24,896]{2,1,0:T(8,128)(2,1)S(1)}, u32[]{:S(2)}, u32[]{:S(2)}) async-start(bf16[4,24,896]{2,1,0:T(8,128)(2,1)} %bitcast.11), calls=%async_computation.3 | async-start | bytes 344064 | tf_op jit(solution)/shard_map/all_to_all | solution.py:77
Sparse Core Ops, SparseCore 0:
  9.5 32.8 all-gather.4
  44.0 30.1 all-gather.6
  77.2 43.8 all-reduce.4
  124.3 28.2 reduce-scatter.4
  155.2 29.0 reduce-scatter.2
where the time goes:
time: 191 us
  waiting for transfers between devices  112 us (59%)
  local copies, waits for them, and re-layouts  29.3 us (15%)
  matrix products  14.6 us (8%)
  starting transfers between devices  14.5 us (8%)
  between operations  14.1 us (7%)
  other arithmetic  5.97 us (3%)
    psum x1, waiting for transfers between devices, body(): lax.psum(jnp.dot(arrived, w_up, preferred_element_type=jnp.float32), 'tp')  44 us
    reduce_scatter x1, waiting for transfers between devices, body(): lax.psum_scatter(part_up.astype(jnp.bfloat16), 'dp', scatter_dimension=1,...  31.7 us
    all_gather x1, waiting for transfers between devices, body(): lax.all_gather(down_weight[0], 'dp', axis=0, tiled=True)  22.8 us
    scatter x1, local copies, waits for them, and re-layouts, place_slots(): jnp.full((experts * capacity,), rows_count, jnp.int32).at[target]  11.8 us
    scatter x1, local copies, waits for them, and re-layouts, place_slots(): jnp.zeros((experts * capacity,), jnp.float32).at[target]  11.8 us
    all_to_all x1, starting transfers between devices, body(): lax.all_to_all(outgoing, 'ctx', split_axis=0, concat_axis=0, tiled=True)  4.26 us
    reduce_scatter x1, waiting for transfers between devices, body(): lax.psum_scatter(part_down.astype(jnp.bfloat16), 'dp', scatter_dimension=...  4.05 us
  transfers between devices with their start and end apart: 9, of which 7 were waited for; matrix products, arithmetic and copies ran while one was open for 23% of the time, Pallas kernels for 0%

commit v1 on v0

--- a/solution.py
+++ b/solution.py
@@ -40,7 +40,9 @@
         lax.all_gather(up_weight[0], "dp", axis=1, tiled=True),
         lax.all_gather(down_weight[0], "dp", axis=0, tiled=True),
     )
-    hidden = lax.psum(jnp.dot(arrived, w_up, preferred_element_type=jnp.float32), "tp")
+    hidden = jnp.sum(
+        lax.all_gather(jnp.dot(arrived, w_up, preferred_element_type=jnp.float32), "tp"), axis=0
+    )
     active = jax.nn.silu(hidden).astype(jnp.bfloat16)
     produced = jnp.dot(active, w_down, preferred_element_type=jnp.float32).astype(jnp.bfloat16)
     returned = lax.all_to_all(

time: 191 us -> 223 us (1.17)
  waiting for transfers between devices: 112 us -> 134 us
  blocking collectives: 0 us -> 16.8 us
  starting transfers between devices: 14.5 us -> 6.96 us
    all_gather x0 -> x1, waiting for transfers between devices: none -> 36.2 us  [body(): lax.all_gather(jnp.dot(arrived, w_up, preferred_element_type=jnp.float32)...]
    all_to_all x0 -> x2, blocking collectives: none -> 16.8 us  [the longest x1 9.24 us: body(): lax.all_to_all(outgoing, 'ctx', split_axis=0, concat_axis=0, tiled=True)]
    all_gather x1, waiting for transfers between devices: 22.8 us -> 8.25 us  [body(): lax.all_gather(down_weight[0], 'dp', axis=0, tiled=True)]
    psum x1, waiting for transfers between devices: 44 us -> 35 us  [body(): lax.psum(lax.dot_general(grad_rows, w_down, contract_last, preferred_elem...]
    all_gather x1, waiting for transfers between devices: 0.02 us -> 8.96 us  [body(): lax.all_gather(up_weight[0], 'dp', axis=1, tiled=True)]
    all_to_all x2 -> x0, starting transfers between devices: 7.62 us -> none  [the longest x1 4.26 us: body(): lax.all_to_all(outgoing, 'ctx', split_axis=0, concat_axis=0, tiled=True)]
    all_to_all x2 -> x0, waiting for transfers between devices: 2.27 us -> none  [the longest x1 2.27 us: body(): lax.all_to_all(grad_send.reshape(sources, capacity, features), 'ctx', spl...]
  transfers between devices with their start and end apart: 9 -> 8, of which waited for: 7 -> 8; matrix products, arithmetic and copies ran while one was open for 23% -> 23% of each run, Pallas kernels for 0% -> 0%
where the time goes in v1:
time: 223 us; the launch traced here: 222 us
  waiting for transfers between devices  134 us (60%)
  local copies, waits for them, and re-layouts  28.6 us (13%)
  blocking collectives  16.8 us (8%)
  between operations  14.4 us (6%)
  matrix products  13.6 us (6%)
  other arithmetic  7.85 us (4%)
  starting transfers between devices  6.96 us (3%)
    all_gather x1, waiting for transfers between devices, body(): lax.all_gather(jnp.dot(arrived, w_up, preferred_element_type=jnp.float32)...  36.2 us
    psum x1, waiting for transfers between devices, body(): lax.psum(lax.dot_general(grad_rows, w_down, contract_last, preferred_elem...  35 us
    reduce_scatter x1, waiting for transfers between devices, body(): lax.psum_scatter(part_up.astype(jnp.bfloat16), 'dp', scatter_dimension=1,...  31.7 us
    scatter x1, local copies, waits for them, and re-layouts, place_slots(): jnp.full((experts * capacity,), rows_count, jnp.int32).at[target]  11.8 us
    scatter x1, local copies, waits for them, and re-layouts, place_slots(): jnp.zeros((experts * capacity,), jnp.float32).at[target]  11.8 us
    all_to_all x1, blocking collectives, body(): lax.all_to_all(outgoing, 'ctx', split_axis=0, concat_axis=0, tiled=True)  9.24 us
    all_gather x1, waiting for transfers between devices, body(): lax.all_gather(up_weight[0], 'dp', axis=1, tiled=True)  8.96 us
    all_gather x1, waiting for transfers between devices, body(): lax.all_gather(down_weight[0], 'dp', axis=0, tiled=True)  8.25 us
  transfers between devices with their start and end apart: 8, of which 8 were waited for; matrix products, arithmetic and copies ran while one was open for 23% of the time, Pallas kernels for 0%

profile of v1, /device:TPU:0, one launch (start us, length us, event | category | flops | bytes accessed | tf_op | source)
XLA Modules:
  0.0 222.0 jit_solution(7982316212200654201)
XLA Ops:
  7.2 0.7 all-gather.7.cloned.1.call-update
  8.0 0.7 all-gather.11.cloned.1.call-update
  9.8 1.2 reduce-window.6
  10.9 0.2 slice_reduce_fusion
  11.6 11.8 %scatter_custom_fusion = s32[96]{0:T(128)S(1)} fusion(s32[3072]{0:T(1024)S(1)} %bitcast.67, s32[3072]{0:T(1024)S(1)} %add_select_fusion, s32[]{:T(128)} %constant.16.clone.1), kind=kCustom, calls=%fused_computation.56 | custom fusion | bytes 388 | tf_op jit(solution)/shard_map/scatter | solution.py:17
  23.4 0.8 gather_fusion
  24.2 9.2 %all_to_all.20 = bf16[4,24,896]{2,1,0:T(8,128)(2,1)S(1)} all-to-all(bf16[4,24,896]{2,1,0:T(8,128)(2,1)S(1)} %bitcast.65), channel_id=1, replica_groups=mesh['ctx'=4,'tp'=4,'dp'=2] {'ctx'}, dimensions={0} | all-to-all | bytes 344064 | tf_op jit(solution)/shard_map/all_to_all | solution.py:36
  33.5 9.0 %all-gather.7.cloned.1.call-done = bf16[1,896,1024]{2,1,0:T(8,128)(2,1)} async-done(((bf16[1,896,512]{2,1,0:T(8,128)(2,1)}), bf16[1,896,1024]{2,1,0:T(8,128)(2,1)}) %all-gather.7.cloned.1.call-update) | async-done | bytes 1835024 | tf_op jit(solution)/shard_map/all_gather | solution.py:40
  42.4 2.7 %fusion.6 = f32[96,1024]{1,0:T(8,128)} fusion(bf16[96,896]{1,0:T(8,128)(2,1)S(1)} %bitcast.58, bf16[1,896,1024]{2,1,0:T(8,128)(2,1)} %all-gather.7.cloned.1.call-done), kind=kOutput, calls=%fused_computation.12 | convolution fusion | flops 176160768 | bytes 2400256 | tf_op jit(solution)/shard_map/dot_general | solution.py:44
  45.5 11.8 %scatter_custom_fusion.1 = f32[96]{0:T(128)S(1)} fusion(s32[3072]{0:T(1024)S(1)} %bitcast.68, f32[3072]{0:T(1024)S(1)} %reshape.139, f32[]{:T(128)} %constant.15.clone.1), kind=kCustom, calls=%fused_computation.54 | custom fusion | bytes 388 | tf_op jit(solution)/shard_map/scatter | solution.py:20
  57.4 0.8 gather_fusion.1
  58.3 7.6 %all_to_all.21 = bf16[4,24,896]{2,1,0:T(8,128)(2,1)S(1)} all-to-all(bf16[4,24,896]{2,1,0:T(8,128)(2,1)S(1)} %fusion.19), channel_id=1, replica_groups=mesh['ctx'=4,'tp'=4,'dp'=2] {'ctx'}, dimensions={0} | all-to-all | bytes 344064 | tf_op jit(solution)/shard_map/all_to_all | solution.py:63
  65.9 8.2 %all-gather.11.cloned.1.call-done = bf16[1,1024,896]{2,1,0:T(8,128)(2,1)} async-done(((bf16[1,512,896]{2,1,0:T(8,128)(2,1)}), bf16[1,1024,896]{2,1,0:T(8,128)(2,1)}) %all-gather.11.cloned.1.call-update) | async-done | bytes 1835024 | tf_op jit(solution)/shard_map/all_gather | solution.py:41
  74.1 2.9 %fusion = f32[96,1024]{1,0:T(8,128)} fusion(bf16[96,896]{1,0:T(8,128)(2,1)S(1)} %bitcast.60, bf16[1,1024,896]{2,1,0:T(8,128)(2,1)} %all-gather.11.cloned.1.call-done), kind=kOutput, calls=%fused_computation.6 | convolution fusion | flops 176160768 | bytes 2400256 | tf_op jit(solution)/shard_map/dot_general | solution.py:73
  77.2 36.2 %all-gather.9.cloned.1.call-done = f32[384,1024]{1,0:T(8,128)} async-done(((f32[96,1024]{1,0:T(8,128)}), f32[384,1024]{1,0:T(8,128)}) %all-gather.9.cloned.1.call-update) | async-done | bytes 1572880 | tf_op jit(solution)/shard_map/all_gather | solution.py:44
  113.4 1.6 reduce_sum.22
  114.9 2.0 convolution_convert_fusion
  116.9 35.0 %all-reduce.4.cloned.1.call-done = f32[96,1024]{1,0:T(8,128)} async-done(((f32[96,1024]{1,0:T(8,128)}), f32[96,1024]{1,0:T(8,128)}) %all-reduce.4.cloned.1.call-update) | async-done | bytes 393232 | tf_op jit(solution)/shard_map/psum | solution.py:72
  152.0 1.1 multiply_convert_fusion
  153.1 2.0 convolution_convert_fusion.1
  155.1 2.8 %fusion.11 = bf16[96,896]{1,0:T(8,128)(2,1)} fusion(bf16[1,1024,896]{2,1,0:T(8,128)(2,1)} %all-gather.11.cloned.1.call-done, f32[96,1024]{1,0:T(8,128)S(1)} %reduce_sum.22), kind=kOutput, calls=%fused_computation.19 | convolution fusion | flops 176738304 | bytes 2400256 | tf_op jit(solution)/shard_map/dot_general | solution.py:47
  157.9 3.4 %all-to-all-start.1 = ((bf16[4,24,896]{2,1,0:T(8,128)(2,1)}), bf16[4,24,896]{2,1,0:T(8,128)(2,1)S(1)}, u32[]{:S(2)}, u32[]{:S(2)}) async-start(bf16[4,24,896]{2,1,0:T(8,128)(2,1)} %bitcast.8), calls=%async_computation.1 | async-start | bytes 344064 | tf_op jit(solution)/shard_map/all_to_all | solution.py:48
  161.3 1.3 fusion.8
  162.6 3.6 %all-to-all-done.1 = bf16[4,24,896]{2,1,0:T(8,128)(2,1)S(1)} async-done(((bf16[4,24,896]{2,1,0:T(8,128)(2,1)}), bf16[4,24,896]{2,1,0:T(8,128)(2,1)S(1)}, u32[]{:S(2)}, u32[]{:S(2)}) %all-to-all-start.1) | async-done | bytes 172064 | tf_op jit(solution)/shard_map/all_to_all | solution.py:48
  166.3 3.4 %all-to-all-start.3 = ((bf16[4,24,896]{2,1,0:T(8,128)(2,1)}), bf16[4,24,896]{2,1,0:T(8,128)(2,1)S(1)}, u32[]{:S(2)}, u32[]{:S(2)}) async-start(bf16[4,24,896]{2,1,0:T(8,128)(2,1)} %bitcast.12), calls=%async_computation.3 | async-start | bytes 344064 | tf_op jit(solution)/shard_map/all_to_all | solution.py:79
  169.6 1.8 scatter_custom_fusion.2
  171.4 0.9 slice.29
  172.3 2.3 %all-to-all-done.3 = bf16[4,24,896]{2,1,0:T(8,128)(2,1)S(1)} async-done(((bf16[4,24,896]{2,1,0:T(8,128)(2,1)}), bf16[4,24,896]{2,1,0:T(8,128)(2,1)S(1)}, u32[]{:S(2)}, u32[]{:S(2)}) %all-to-all-start.3) | async-done | bytes 172064 | tf_op jit(solution)/shard_map/all_to_all | solution.py:79
  174.6 1.7 scatter_custom_fusion.3
  176.3 0.9 slice.28
  177.3 6.2 %reduce-scatter.5.cloned.1.call-done = bf16[512,896]{1,0:T(8,128)(2,1)} async-done(((bf16[1024,896]{1,0:T(8,128)(2,1)}), bf16[512,896]{1,0:T(8,128)(2,1)}) %reduce-scatter.5.cloned.1.call-update) | async-done | bytes 917520 | tf_op jit(solution)/shard_map/reduce_scatter | solution.py:96
  183.5 31.7 %reduce-scatter.3.cloned.1.call-done = bf16[896,512]{1,0:T(8,128)(2,1)} async-done(((bf16[896,1024]{1,0:T(8,128)(2,1)}), bf16[896,512]{1,0:T(8,128)(2,1)}) %reduce-scatter.3.cloned.1.call-update) | async-done | bytes 917520 | tf_op jit(solution)/shard_map/reduce_scatter | solution.py:93
  (44 shorter events, 2.2 us)
Async XLA Ops:
  7.2 1.6 copy-start.3
  7.2 4.2 %copy-start.1 = (bf16[384,896]{1,0:T(8,128)(2,1)S(1)}, bf16[384,896]{1,0:T(8,128)(2,1)}, u32[]{:S(2)}) copy-start(bf16[384,896]{1,0:T(8,128)(2,1)} %param.6) | copy-start | bytes 2064388
  7.2 35.2 %all-gather.7.cloned.1.call-start = ((), (), s32[]{:S(2)}) async-start(), calls=%async_computation.9 | async-start | bytes 2752512 | tf_op jit(solution)/shard_map/all_gather | solution.py:40
  7.9 66.2 %all-gather.11.cloned.1.call-start = ((), (), s32[]{:S(2)}) async-start(), calls=%async_computation.11 | async-start | bytes 2752512 | tf_op jit(solution)/shard_map/all_gather | solution.py:41
  8.7 104.7 %all-gather.9.cloned.1.call-start = ((), (), s32[]{:S(2)}) async-start(), calls=%async_computation.10 | async-start | bytes 1966080 | tf_op jit(solution)/shard_map/all_gather | solution.py:44
  24.2 21.0 %copy-start.4 = (s32[384,8]{0,1:T(8,128)S(1)}, s32[384,8]{0,1:T(8,128)}, u32[]{:S(2)}) copy-start(s32[384,8]{0,1:T(8,128)} %param.8) | copy-start | bytes 36868
  24.2 33.1 %copy-start.2 = (bf16[384,896]{1,0:T(8,128)(2,1)S(1)}, bf16[384,896]{1,0:T(8,128)(2,1)}, u32[]{:S(2)}) copy-start(bf16[384,896]{1,0:T(8,128)(2,1)} %param.11) | copy-start | bytes 2064388
  45.2 106.8 %all-reduce.4.cloned.1.call-start = ((), (), s32[]{:S(2)}) async-start(), calls=%async_computation.6 | async-start | bytes 786432 | tf_op jit(solution)/shard_map/psum | solution.py:72
  77.1 106.4 %reduce-scatter.5.cloned.1.call-start = ((), (), s32[]{:S(2)}) async-start(), calls=%async_computation.8 | async-start | bytes 2752512 | tf_op jit(solution)/shard_map/reduce_scatter | solution.py:96
  116.9 98.3 %reduce-scatter.3.cloned.1.call-start = ((), (), s32[]{:S(2)}) async-start(), calls=%async_computation.7 | async-start | bytes 2752512 | tf_op jit(solution)/shard_map/reduce_scatter | solution.py:93
  155.1 6.1 %copy-start = (bf16[1,896,1024]{2,1,0:T(8,128)(2,1)S(1)}, bf16[1,896,1024]{2,1,0:T(8,128)(2,1)}, u32[]{:S(2)}) copy-start(bf16[1,896,1024]{2,1,0:T(8,128)(2,1)} %all-gather.7.cloned.1.call-done) | copy-start | bytes 5505028
  157.9 8.4 %all-to-all-start.1 = ((bf16[4,24,896]{2,1,0:T(8,128)(2,1)}), bf16[4,24,896]{2,1,0:T(8,128)(2,1)S(1)}, u32[]{:S(2)}, u32[]{:S(2)}) async-start(bf16[4,24,896]{2,1,0:T(8,128)(2,1)} %bitcast.8), calls=%async_computation.1 | async-start | bytes 344064 | tf_op jit(solution)/shard_map/all_to_all | solution.py:48
  166.3 8.4 %all-to-all-start.3 = ((bf16[4,24,896]{2,1,0:T(8,128)(2,1)}), bf16[4,24,896]{2,1,0:T(8,128)(2,1)S(1)}, u32[]{:S(2)}, u32[]{:S(2)}) async-start(bf16[4,24,896]{2,1,0:T(8,128)(2,1)} %bitcast.12), calls=%async_computation.3 | async-start | bytes 344064 | tf_op jit(solution)/shard_map/all_to_all | solution.py:79
Sparse Core Ops, SparseCore 0:
  9.5 32.8 all-gather.6
  44.0 30.1 all-gather.10
  76.3 37.0 all-gather.8
  116.1 35.8 all-reduce.3
  154.7 28.7 reduce-scatter.4
  186.1 28.9 reduce-scatter.2
